TPU v7x, 32 devices: a whole 2x2x4 slice. The times are simulated.
32 devices in a mesh: dp: 16 (over z, x, core), tensor: 2 (over y).
Axes of the slice: x: 2, y: 2, z: 4, core: 2. Of those that a mesh axis runs over, the one named last changes fastest.
Arguments:
- tokens: bfloat16 [32768, 512], P('dp'), may hold values from -6 to 6
- seq_lengths: int32 [32], P('dp'), may hold values from 1024 to 1024, as said below
- packed_slot: int32 [32768], P('dp'), may hold values from 0 to 32767, as said below
- out_grad: bfloat16 [32768, 512], P('dp'), may hold values from -6 to 6
- qkv_weight: bfloat16 [3, 512, 512], P(None, None, 'tensor'), may hold values from -0.25 to 0.25
- out_weight: bfloat16 [512, 512], P('tensor'), may hold values from -2 to 2
- up_weight: bfloat16 [512, 2048], P(None, 'tensor'), may hold values from -0.25 to 0.25
- down_weight: bfloat16 [2048, 512], P('tensor'), may hold values from -0.125 to 0.125
- gain_first: float32 [512], replicated, may hold values from 0.1 to 1.9
- shift_first: float32 [512], replicated, may hold values from -0.6 to 0.6
- gain_second: float32 [512], replicated, may hold values from 0.1 to 1.9
- shift_second: float32 [512], replicated, may hold values from -0.6 to 0.6
- up_bias: float32 [2048], P('tensor'), may hold values from -12 to 12
Outputs:
- layer_out: bfloat16 [32768, 512], P('dp')
- grad_input: bfloat16 [32768, 512], P('dp')
- grad_qkv: float32 [3, 512, 512], P(None, None, 'tensor')
- grad_outproj: float32 [512, 512], P('tensor')
- grad_up: float32 [512, 2048], P(None, 'tensor')
- grad_down: float32 [2048, 512], P('tensor')
- grad_gain_first: float32 [512], replicated
- grad_shift_first: float32 [512], replicated
- grad_gain_second: float32 [512], replicated
- grad_shift_second: float32 [512], replicated
- grad_up_bias: float32 [2048], P('tensor')
Inputs may be any that keep to these rules, and one draw needn't show every extreme that they name: Each pair seq_lengths[2b], seq_lengths[2b+1] sums to 2048; every length is a multiple of 64; some pair is (1024, 1024). packed_slot is a permutation of the rows; of the 2048 rows of one index of dp, exactly 128 have packed_slot // 2048 equal to each index of dp.
All inputs are finite; a program needn't handle non-finite values.
Results may differ from a plain program's by a relative error of at most 0.015.
Values may be sent and summed in bfloat16 or wider, within the bound.
No kernel may reach another device: no remote copies, remote signals or barrier semaphores. Data moves between devices by JAX's collectives and lax.ppermute only.
A program may use at most 192 MiB of HBM per device.

v0:
```python
import jax
import jax.numpy as jnp
from jax import lax
from jax.sharding import PartitionSpec as P

HD = 64
BLK = 64


def layer_norm(value, gain, shift):
    mean = jnp.mean(value, axis=-1, keepdims=True)
    cent = value - mean
    var = jnp.mean(cent * cent, axis=-1, keepdims=True)
    return cent * lax.rsqrt(var + 1e-05) * gain + shift


def feature(value):
    return jnp.where(value > 0, value + 1.0, jnp.exp(jnp.minimum(value, 0.0)))


def feature_slope(value):
    return jnp.where(value > 0, 1.0, jnp.exp(jnp.minimum(value, 0.0)))


def silu_slope(value):
    sigma = jax.nn.sigmoid(value)
    return sigma * (1.0 + value * (1.0 - sigma))


def rounded(value):
    return lax.optimization_barrier(value.astype(jnp.bfloat16)).astype(jnp.float32)


def linear_attention(q_feat, k_feat, v_feat, stretch_seq):
    best = lax.Precision.HIGHEST
    nblk = q_feat.shape[0] // BLK
    query = q_feat.reshape(nblk, BLK, -1, HD)
    keys = k_feat.reshape(nblk, BLK, -1, HD)
    values = v_feat.reshape(nblk, BLK, -1, HD)
    outer = jnp.einsum("cjhe,cjhf->chef", keys, values, precision=best)
    ksum = jnp.sum(keys, axis=1)
    index = jnp.arange(nblk)
    mixing = (
        (index[None, :] < index[:, None]) & (stretch_seq[None, :] == stretch_seq[:, None])
    ).astype(jnp.float32)
    state = jnp.einsum("cd,dhef->chef", mixing, outer, precision=best)
    zsum = jnp.einsum("cd,dhe->che", mixing, ksum, precision=best)
    scores = jnp.einsum("cihe,cjhe->chij", query, keys, precision=best)
    lower = (jnp.arange(BLK)[None, :] <= jnp.arange(BLK)[:, None]).astype(jnp.float32)
    scores = scores * lower
    numer = jnp.einsum("cihe,chef->cihf", query, state, precision=best)
    numer = numer + jnp.einsum("chij,cjhf->cihf", scores, values, precision=best)
    denom = jnp.einsum("cihe,che->cih", query, zsum, precision=best)
    denom = denom + jnp.transpose(jnp.sum(scores, axis=-1), (0, 2, 1)) + 1e-06
    result = numer / denom[..., None]
    return result.reshape(nblk * BLK, -1)


def per_device(
    tokens,
    seq_lengths,
    packed_slot,
    out_grad,
    qkv_weight,
    out_weight,
    up_weight,
    down_weight,
    gain_first,
    shift_first,
    gain_second,
    shift_second,
    up_bias,
):
    rows = tokens.shape[0]
    count = lax.axis_size("dp")
    slot = rows // count
    order = jnp.argsort(packed_slot)
    sent = (
        tokens[order].reshape(count, slot, -1),
        out_grad[order].reshape(count, slot, -1),
        packed_slot[order].reshape(count, slot),
    )
    got_rows, got_grads, got_slots = (
        lax.all_to_all(sent[0], "dp", split_axis=0, concat_axis=0, tiled=True),
        lax.all_to_all(sent[1], "dp", split_axis=0, concat_axis=0, tiled=True),
        lax.all_to_all(sent[2], "dp", split_axis=0, concat_axis=0, tiled=True),
    )
    local_pos = got_slots.reshape(rows) % rows
    arrange = jnp.argsort(local_pos)
    inputs = got_rows.reshape(rows, -1)[arrange].astype(jnp.float32)
    grad_low = got_grads.reshape(rows, -1)[arrange]
    nblk = rows // BLK
    stretch_seq = (jnp.arange(nblk) * BLK >= seq_lengths[0]).astype(jnp.int32)
    first, first_pull = jax.vjp(layer_norm, inputs, gain_first, shift_first)
    first_low = first.astype(jnp.bfloat16)
    projected = jnp.einsum("td,jdc->jtc", first_low, qkv_weight, preferred_element_type=jnp.float32)
    q_feat = rounded(feature(projected[0]))
    k_feat = rounded(feature(projected[1]))
    v_feat = rounded(projected[2])
    attended, attn_pull = jax.vjp(
        lambda a, b, c: linear_attention(a, b, c, stretch_seq), q_feat, k_feat, v_feat
    )
    attended_low = attended.astype(jnp.bfloat16)
    attn_part = jnp.dot(attended_low, out_weight, preferred_element_type=jnp.float32)
    middle = inputs + lax.psum(attn_part.astype(jnp.bfloat16), "tensor").astype(jnp.float32)
    second, second_pull = jax.vjp(layer_norm, middle, gain_second, shift_second)
    second_low = second.astype(jnp.bfloat16)
    hidden = jnp.dot(second_low, up_weight, preferred_element_type=jnp.float32) + up_bias
    active_low = jax.nn.silu(hidden).astype(jnp.bfloat16)
    ffn_part = jnp.dot(active_low, down_weight, preferred_element_type=jnp.float32)
    result = (
        middle + lax.psum(ffn_part.astype(jnp.bfloat16), "tensor").astype(jnp.float32)
    ).astype(jnp.bfloat16)
    grad_down = jnp.einsum("tf,td->fd", active_low, grad_low, preferred_element_type=jnp.float32)
    grad_active = jnp.einsum("td,fd->tf", grad_low, down_weight, preferred_element_type=jnp.float32)
    grad_hidden = (grad_active * silu_slope(hidden)).astype(jnp.bfloat16)
    grad_up = jnp.einsum("td,tf->df", second_low, grad_hidden, preferred_element_type=jnp.float32)
    grad_up_bias = jnp.sum(grad_hidden.astype(jnp.float32), axis=0)
    second_part = jnp.einsum(
        "tf,df->td", grad_hidden, up_weight, preferred_element_type=jnp.float32
    )
    grad_second = lax.psum(second_part.astype(jnp.bfloat16), "tensor").astype(jnp.float32)
    middle_norm, grad_gain_second, grad_shift_second = second_pull(grad_second)
    grad_middle = grad_low.astype(jnp.float32) + middle_norm
    middle_low = grad_middle.astype(jnp.bfloat16)
    grad_outproj = jnp.einsum(
        "tc,td->cd", attended_low, middle_low, preferred_element_type=jnp.float32
    )
    grad_attended = jnp.einsum(
        "td,cd->tc", middle_low, out_weight, preferred_element_type=jnp.float32
    )
    grad_qf, grad_kf, grad_vf = attn_pull(grad_attended)
    grad_proj = jnp.stack(
        [grad_qf * feature_slope(projected[0]), grad_kf * feature_slope(projected[1]), grad_vf]
    ).astype(jnp.bfloat16)
    grad_qkv = jnp.einsum("td,jtc->jdc", first_low, grad_proj, preferred_element_type=jnp.float32)
    first_part = jnp.einsum(
        "jtc,jdc->td", grad_proj, qkv_weight, preferred_element_type=jnp.float32
    )
    grad_first = lax.psum(first_part.astype(jnp.bfloat16), "tensor").astype(jnp.float32)
    input_norm, grad_gain_first, grad_shift_first = first_pull(grad_first)
    grad_inputs = (grad_middle + input_norm).astype(jnp.bfloat16)
    (
        grad_qkv,
        grad_outproj,
        grad_up,
        grad_down,
        grad_up_bias,
        grad_gain_first,
        grad_shift_first,
        grad_gain_second,
        grad_shift_second,
    ) = lax.psum(
        (
            grad_qkv,
            grad_outproj,
            grad_up,
            grad_down,
            grad_up_bias,
            grad_gain_first,
            grad_shift_first,
            grad_gain_second,
            grad_shift_second,
        ),
        "dp",
    )
    back = (
        result[local_pos].reshape(count, slot, -1),
        grad_inputs[local_pos].reshape(count, slot, -1),
    )
    got_out, got_input = (
        lax.all_to_all(back[0], "dp", split_axis=0, concat_axis=0, tiled=True),
        lax.all_to_all(back[1], "dp", split_axis=0, concat_axis=0, tiled=True),
    )
    undo = jnp.argsort(order)
    layer_out = got_out.reshape(rows, -1)[undo]
    grad_input = got_input.reshape(rows, -1)[undo]
    return (
        layer_out,
        grad_input,
        grad_qkv,
        grad_outproj,
        grad_up,
        grad_down,
        grad_gain_first,
        grad_shift_first,
        grad_gain_second,
        grad_shift_second,
        grad_up_bias,
    )


def solution(mesh):
    placed = (
        P("dp", None),
        P("dp"),
        P("dp"),
        P("dp", None),
        P(None, None, "tensor"),
        P("tensor", None),
        P(None, "tensor"),
        P("tensor", None),
        P(),
        P(),
        P(),
        P(),
        P("tensor"),
    )
    return jax.shard_map(
        per_device,
        mesh=mesh,
        in_specs=placed,
        out_specs=(
            P("dp", None),
            P("dp", None),
            P(None, None, "tensor"),
            P("tensor", None),
            P(None, "tensor"),
            P("tensor", None),
            P(),
            P(),
            P(),
            P(),
            P("tensor"),
        ),
        check_vma=False,
    )
```

profile of v0, /device:TPU:0, one launch (start us, length us, event | category | flops | bytes accessed | tf_op | source)
XLA Modules:
  0.0 935.9 jit_solution(12726560406458529215)
XLA Ops:
  13.1 20.6 %gather_fusion.1 = s32[2048]{0:T(1024)} fusion(s32[2048]{0:T(1024)S(1)} %copy-done.2, s32[2048]{0:T(1024)S(1)} %fusion.86), kind=kCustom, calls=%fused_computation.1 | custom fusion | bytes 24576 | tf_op jit(solution)/shard_map/gather | solution.py:81
  33.7 7.4 all-to-all-start.1
  41.0 9.2 gather_fusion
  56.3 11.1 %gather_fusion.5 = bf16[2048,512]{1,0:T(8,128)(2,1)} fusion(bf16[2048,512]{1,0:T(8,128)(2,1)} %param.16, s32[2048]{0:T(1024)S(1)} %fusion.86), kind=kCustom, calls=%fused_computation.5 | custom fusion | bytes 4202496 | tf_op jit(solution)/shard_map/gather | solution.py:80
  72.5 24.8 %all-to-all-done = bf16[16,128,512]{2,1,0:T(8,128)(2,1)S(1)} async-done(((bf16[16,128,512]{2,1,0:T(8,128)(2,1)}), bf16[16,128,512]{2,1,0:T(8,128)(2,1)S(1)}, u32[]{:S(2)}, u32[]{:S(2)}) %all-to-all-start) | async-done | bytes 2097184 | tf_op jit(solution)/shard_map/all_to_all | solution.py:84
  97.4 11.3 %all-to-all-start.3 = ((bf16[16,128,512]{2,1,0:T(8,128)(2,1)}), bf16[16,128,512]{2,1,0:T(8,128)(2,1)}, u32[]{:S(2)}, u32[]{:S(2)}) async-start(bf16[16,128,512]{2,1,0:T(8,128)(2,1)} %bitcast.114), calls=%async_computation.3 | async-start | bytes 4194304 | tf_op jit(solution)/shard_map/all_to_all | solution.py:85
  108.9 9.5 %gather_fusion.2 = bf16[2048,512]{1,0:T(8,128)(2,1)S(1)} fusion(bf16[2048,512]{1,0:T(8,128)(2,1)} %bitcast.113, s32[2048]{0:T(1024)S(1)} %fusion.87), kind=kCustom, calls=%fused_computation.2 | custom fusion | bytes 4202496 | tf_op jit(solution)/shard_map/gather | solution.py:90
  158.4 7.2 fusion.29
  178.8 11.3 %gather_fusion.6 = bf16[2048,512]{1,0:T(8,128)(2,1)} fusion(bf16[2048,512]{1,0:T(8,128)(2,1)} %bitcast.22, s32[2048]{0:T(1024)S(1)} %fusion.87), kind=kCustom, calls=%fused_computation.6 | custom fusion | bytes 4202496 | tf_op jit(solution)/shard_map/gather | solution.py:91
  190.1 53.0 %all-reduce.8.cloned.1.call-done = bf16[2048,512]{1,0:T(8,128)(2,1)} async-done(((bf16[2048,512]{1,0:T(8,128)(2,1)}), bf16[2048,512]{1,0:T(8,128)(2,1)}) %all-reduce.8.cloned.1.call-update) | async-done | bytes 2097168 | tf_op jit(solution)/shard_map/psum | solution.py:105
  269.5 56.8 %all-reduce.10.cloned.1.call-done = bf16[2048,512]{1,0:T(8,128)(2,1)} async-done(((bf16[2048,512]{1,0:T(8,128)(2,1)}), bf16[2048,512]{1,0:T(8,128)(2,1)}) %all-reduce.10.cloned.1.call-update) | async-done | bytes 2097168 | tf_op jit(solution)/shard_map/psum | solution.py:122
  343.6 15.5 %fusion.15 = f32[32,4,64,64]{3,2,1,0:T(8,128)} fusion(f32[32,4,64,64]{2,3,1,0:T(8,128)} %copy-done.30, f32[64,64]{0,1:T(8,128)S(1)} %fusion.79, f32[32,64,4,64]{1,0,3,2:T(8,128)} %reshape.276, f32[32,64,4]{1,2,0:T(4,128)S(1)} %copy-done.53), kind=kOutput, calls=%fused_computation.41 | convolution fusion | flops 403701760 | bytes 6340608 | tf_op jit(solution)/shard_map/transpose(jvp(chij,cjhf->cihf))/dot_general | solution.py:52
  359.1 13.6 %fusion.21 = f32[32,4,64,64]{2,3,1,0:T(8,128)} fusion(f32[32,4,64,64]{3,0,2,1:T(8,128)S(1)} %copy-done.22, f32[32,64,4,64]{1,0,3,2:T(8,128)S(1)} %copy-done.23, f32[32,64,4]{1,2,0:T(4,128)S(1)} %copy-done.53), kind=kOutput, calls=%fused_computation.47 | convolution fusion | flops 403177472 | bytes 6324224 | tf_op jit(solution)/shard_map/transpose(jvp(cihe,chef->cihf))/dot_general | solution.py:51
  379.5 7.5 fusion.19
  437.9 9.9 %add_bitcast_fusion = f32[32,64,4,64]{1,3,2,0:T(8,128)} fusion(f32[32,4,64,64]{2,3,1,0:T(8,128)} %fusion.21, f32[32,4,64,64]{2,3,1,0:T(8,128)} %fusion.19, f32[32,4,64]{2,1,0:T(4,128)S(1)} %copy.105, f32[32,4,64]{2,1,0:T(4,128)S(1)} %get-tuple-element.83, f32[64,64]{0,1:T(8,128)S(1)} %fusion.79, bf16[32,64,4,64]{3,2,1,0:T(4,128)(2,1)} %reshape.267), kind=kOutput, calls=%fused_computation.59 | convolution fusion | flops 405274624 | bytes 7421952 | tf_op jit(solution)/shard_map/transpose(jvp(cihe,cjhe->chij))/dot_general | solution.py:48
  468.5 107.7 %all-reduce.14.cloned.1.call-done = (bf16[2048,512]{1,0:T(8,128)(2,1)}, bf16[2048,512]{1,0:T(8,128)(2,1)}) async-done(((bf16[2048,512]{1,0:T(8,128)(2,1)}, bf16[2048,512]{1,0:T(8,128)(2,1)}), (bf16[2048,512]{1,0:T(8,128)(2,1)}, bf16[2048,512]{1,0:T(8,128)(2,1)})) %all-reduce.14.cloned.1.call-update) | async-done | bytes 4194320 | tf_op jit(solution)/shard_map/psum | solution.py:112
  589.1 11.1 %gather_fusion.7 = bf16[2048,512]{1,0:T(8,128)(2,1)} fusion(bf16[2048,512]{1,0:T(8,128)(2,1)} %get-tuple-element.80, s32[2048]{0:T(1024)S(1)} %broadcast_clamp_fusion), kind=kCustom, calls=%fused_computation.7 | custom fusion | bytes 4202496 | tf_op jit(solution)/shard_map/gather | solution.py:169
  616.9 11.1 %gather_fusion.3 = bf16[2048,512]{1,0:T(8,128)(2,1)} fusion(bf16[2048,512]{1,0:T(8,128)(2,1)} %get-tuple-element.81, s32[2048]{0:T(1024)S(1)} %broadcast_clamp_fusion), kind=kCustom, calls=%fused_computation.3 | custom fusion | bytes 4202496 | tf_op jit(solution)/shard_map/gather | solution.py:168
  628.0 19.3 %all-to-all-done.4 = bf16[16,128,512]{2,1,0:T(8,128)(2,1)} async-done(((bf16[16,128,512]{2,1,0:T(8,128)(2,1)}), bf16[16,128,512]{2,1,0:T(8,128)(2,1)}, u32[]{:S(2)}, u32[]{:S(2)}) %all-to-all-start.4) | async-done | bytes 2097184 | tf_op jit(solution)/shard_map/all_to_all | solution.py:173
  647.3 11.3 %all-to-all-start.2 = ((bf16[16,128,512]{2,1,0:T(8,128)(2,1)}), bf16[16,128,512]{2,1,0:T(8,128)(2,1)}, u32[]{:S(2)}, u32[]{:S(2)}) async-start(bf16[16,128,512]{2,1,0:T(8,128)(2,1)} %bitcast.115), calls=%async_computation.2 | async-start | bytes 4194304 | tf_op jit(solution)/shard_map/all_to_all | solution.py:172
  672.6 164.9 %all-reduce.12.cloned.1.call-done = (f32[3,512,256]{1,2,0:T(8,128)}, f32[256,512]{1,0:T(8,128)}, f32[512,1024]{1,0:T(8,128)}, f32[1024,512]{1,0:T(8,128)}) async-done(((f32[3,512,256]{1,2,0:T(8,128)}, f32[256,512]{1,0:T(8,128)}, f32[512,1024]{1,0:T(8,128)}, f32[1024,512]{1,0:T(8,128)}), (f32[3,512,256]{1,2,0:T(8,128)}, f32[256,512]{1,0:T(8,128)}, f32[512,1024]{1,0:T(8,128)}, ...) | async-done | bytes 6291472 | tf_op jit(solution)/shard_map/psum | solution.py:153
  840.6 60.4 %all-reduce = (f32[512]{0:T(512)}, f32[512]{0:T(512)}, f32[512]{0:T(512)}, f32[512]{0:T(512)}, f32[1024]{0:T(1024)}) all-reduce(f32[512]{0:T(512)S(1)} %get-tuple-element.52, f32[512]{0:T(512)S(1)} %get-tuple-element.55, f32[512]{0:T(512)S(1)} %get-tuple-element.50, ...), channel_id=1, replica_groups=mesh['dp'=16,'tensor'=2] {'dp'}, use_global_device_ids=true, to_apply=%region_23.24 | all-reduce | flops 3072 | bytes 24576 | tf_op jit(solution)/shard_map/psum | solution.py:153
  901.0 11.1 %gather_fusion.8 = bf16[2048,512]{1,0:T(8,128)(2,1)} fusion(bf16[2048,512]{1,0:T(8,128)(2,1)} %bitcast.37, s32[2048]{0:T(1024)S(1)} %fusion.88), kind=kCustom, calls=%fused_computation.8 | custom fusion | bytes 4202496 | tf_op jit(solution)/shard_map/gather | solution.py:177
  912.1 11.2 %gather_fusion.4 = bf16[2048,512]{1,0:T(8,128)(2,1)} fusion(bf16[2048,512]{1,0:T(8,128)(2,1)} %bitcast.20, s32[2048]{0:T(1024)S(1)} %fusion.88), kind=kCustom, calls=%fused_computation.4 | custom fusion | bytes 4202496 | tf_op jit(solution)/shard_map/gather | solution.py:176
  (237 shorter events, 244.2 us)
Async XLA Ops:
  7.2 33.9 %copy-start = (bf16[2048,512]{1,0:T(8,128)(2,1)S(1)}, bf16[2048,512]{1,0:T(8,128)(2,1)}, u32[]{:S(2)}) copy-start(bf16[2048,512]{1,0:T(8,128)(2,1)} %param.13) | copy-start | bytes 6291460
  13.1 20.6 %copy-start.54 = (s32[2048]{0:T(1024)}, s32[2048]{0:T(1024)S(1)}, u32[]{:S(2)}) copy-start(s32[2048]{0:T(1024)S(1)} %get-tuple-element.14) | copy-start | bytes 24580
  33.7 16.6 %all-to-all-start.1 = ((s32[16,1,128]{2,1,0:T(1,128)}), s32[16,1,128]{2,1,0:T(1,128)S(1)}, u32[]{:S(2)}, u32[]{:S(2)}) async-start(s32[16,1,128]{2,1,0:T(1,128)} %bitcast.2), calls=%async_computation.1 | async-start | bytes 16384 | tf_op jit(solution)/shard_map/all_to_all | solution.py:86
  50.2 17.2 %copy-start.50 = (s32[16,1,128]{2,1,0:T(1,128)}, s32[16,1,128]{2,1,0:T(1,128)S(1)}, u32[]{:S(2)}) copy-start(s32[16,1,128]{2,1,0:T(1,128)S(1)} %all-to-all-done.1) | copy-start | bytes 24580
  50.2 47.1 %all-to-all-start = ((bf16[16,128,512]{2,1,0:T(8,128)(2,1)}), bf16[16,128,512]{2,1,0:T(8,128)(2,1)S(1)}, u32[]{:S(2)}, u32[]{:S(2)}) async-start(bf16[16,128,512]{2,1,0:T(8,128)(2,1)} %bitcast.116), calls=%async_computation | async-start | bytes 4194304 | tf_op jit(solution)/shard_map/all_to_all | solution.py:84
  97.4 81.4 %all-to-all-start.3 = ((bf16[16,128,512]{2,1,0:T(8,128)(2,1)}), bf16[16,128,512]{2,1,0:T(8,128)(2,1)}, u32[]{:S(2)}, u32[]{:S(2)}) async-start(bf16[16,128,512]{2,1,0:T(8,128)(2,1)} %bitcast.114), calls=%async_computation.3 | async-start | bytes 4194304 | tf_op jit(solution)/shard_map/all_to_all | solution.py:85
  108.6 134.5 %all-reduce.8.cloned.1.call-start = ((), (), s32[]{:S(2)}) async-start(), calls=%async_computation.5 | async-start | bytes 4194304 | tf_op jit(solution)/shard_map/psum | solution.py:105
  178.8 147.6 %all-reduce.10.cloned.1.call-start = ((), (), s32[]{:S(2)}) async-start(), calls=%async_computation.6 | async-start | bytes 4194304 | tf_op jit(solution)/shard_map/psum | solution.py:122
  190.1 56.5 %copy-start.58 = (f32[512]{0:T(512)S(1)}, f32[512]{0:T(512)}, u32[]{:S(2)}) copy-start(f32[512]{0:T(512)} %param.23) | copy-start | bytes 6148
  190.1 56.5 %copy-start.63 = (f32[1024]{0:T(1024)S(1)}, f32[1024]{0:T(1024)}, u32[]{:S(2)}) copy-start(f32[1024]{0:T(1024)} %param.25) | copy-start | bytes 12292
  190.1 56.5 %copy-start.64 = (f32[512]{0:T(512)S(1)}, f32[512]{0:T(512)}, u32[]{:S(2)}) copy-start(f32[512]{0:T(512)} %param.24) | copy-start | bytes 6148
  263.3 312.9 %all-reduce.14.cloned.1.call-start = ((), (), s32[]{:S(2)}) async-start(), calls=%async_computation.8 | async-start | bytes 8388608 | tf_op jit(solution)/shard_map/psum | solution.py:112
  343.6 15.5 %copy-start.22 = (f32[32,4,64,64]{3,0,2,1:T(8,128)S(1)}, f32[32,4,64,64]{3,0,2,1:T(8,128)}, u32[]{:S(2)}) copy-start(f32[32,4,64,64]{3,0,2,1:T(8,128)} %copy-done.21) | copy-start | bytes 6291460
  343.6 15.5 %copy-start.23 = (f32[32,64,4,64]{1,0,3,2:T(8,128)S(1)}, f32[32,64,4,64]{1,0,3,2:T(8,128)}, u32[]{:S(2)}) copy-start(f32[32,64,4,64]{1,0,3,2:T(8,128)} %reshape.276) | copy-start | bytes 6291460
  359.1 13.6 %copy-start.35 = (bf16[32,64,4,64]{1,3,2,0:T(8,128)(2,1)S(1)}, bf16[32,64,4,64]{1,3,2,0:T(8,128)(2,1)}, u32[]{:S(2)}) copy-start(bf16[32,64,4,64]{1,3,2,0:T(8,128)(2,1)} %copy.119) | copy-start | bytes 3145732
  467.7 108.4 %copy-start.45 = (f32[2048]{0:T(1024)S(1)}, f32[2048]{0:T(1024)}, u32[]{:S(2)}) copy-start(f32[2048]{0:T(1024)} %copy-done.44) | copy-start | bytes 24580
  467.7 108.4 %copy-start.57 = (f32[512]{0:T(512)S(1)}, f32[512]{0:T(512)}, u32[]{:S(2)}) copy-start(f32[512]{0:T(512)} %param.21) | copy-start | bytes 6148
  467.7 111.9 %copy-start.49 = (f32[2048]{0:T(1024)S(1)}, f32[2048]{0:T(1024)}, u32[]{:S(2)}) copy-start(f32[2048]{0:T(1024)} %copy-done.48) | copy-start | bytes 24580
  467.7 111.9 %copy-start.47 = (f32[2048]{0:T(1024)S(1)}, f32[2048]{0:T(1024)}, u32[]{:S(2)}) copy-start(f32[2048]{0:T(1024)} %copy-done.46) | copy-start | bytes 24580
  600.2 47.1 %all-to-all-start.4 = ((bf16[16,128,512]{2,1,0:T(8,128)(2,1)}), bf16[16,128,512]{2,1,0:T(8,128)(2,1)}, u32[]{:S(2)}, u32[]{:S(2)}) async-start(bf16[16,128,512]{2,1,0:T(8,128)(2,1)} %bitcast.117), calls=%async_computation.4 | async-start | bytes 4194304 | tf_op jit(solution)/shard_map/all_to_all | solution.py:173
  628.0 30.6 %copy-start.27 = (bf16[2048,256]{0,1:T(8,128)(2,1)S(1)}, bf16[2048,256]{0,1:T(8,128)(2,1)}, u32[]{:S(2)}) copy-start(bf16[2048,256]{0,1:T(8,128)(2,1)} %copy-done.26) | copy-start | bytes 3145732
  628.0 33.7 %copy-start.66 = (f32[512]{0:T(512)S(1)}, f32[512]{0:T(512)}, u32[]{:S(2)}) copy-start(f32[512]{0:T(512)} %param.22) | copy-start | bytes 6148
  647.3 264.8 %all-to-all-start.2 = ((bf16[16,128,512]{2,1,0:T(8,128)(2,1)}), bf16[16,128,512]{2,1,0:T(8,128)(2,1)}, u32[]{:S(2)}, u32[]{:S(2)}) async-start(bf16[16,128,512]{2,1,0:T(8,128)(2,1)} %bitcast.115), calls=%async_computation.2 | async-start | bytes 4194304 | tf_op jit(solution)/shard_map/all_to_all | solution.py:172
  658.6 179.0 %all-reduce.12.cloned.1.call-start = ((), (), s32[]{:S(2)}) async-start(), calls=%async_computation.7 | async-start | bytes 12582912 | tf_op jit(solution)/shard_map/psum | solution.py:153
  (55 other events, 277.9 us)
Sparse Core Ops, SparseCore 0:
  178.9 64.1 all-reduce.7
  263.4 62.9 all-reduce.9
  467.9 108.2 all-reduce.13
  667.0 170.4 all-reduce.11
where the time goes:
time: 941 us; the launch traced here: 936 us
  waiting for transfers between devices  427 us (45%)
  local copies, waits for them, and re-layouts  190 us (20%)
  matrix products  148 us (16%)
  blocking collectives  60.4 us (6%)
  other arithmetic  54 us (6%)
  starting transfers between devices  42.2 us (4%)
  between operations  15.1 us (2%)
    psum x1, waiting for transfers between devices, per_device(): lax.psum((grad_qkv, grad_outproj, grad_up, grad_down, grad_up_bias, grad_...  165 us
    psum x1, waiting for transfers between devices, per_device(): lax.psum(ffn_part.astype(jnp.bfloat16), 'tensor').astype(jnp.float32)  108 us
    psum x1, blocking collectives, per_device(): lax.psum((grad_qkv, grad_outproj, grad_up, grad_down, grad_up_bias, grad_...  60.4 us
    psum x1, waiting for transfers between devices, per_device(): lax.psum(second_part.astype(jnp.bfloat16), 'tensor').astype(jnp.float32)  56.8 us
    psum x1, waiting for transfers between devices, per_device(): lax.psum(attn_part.astype(jnp.bfloat16), 'tensor').astype(jnp.float32)  53 us
    dot_general x3, matrix products, linear_attention(): jnp.einsum('chij,cjhf->cihf', scores, values, precision=best)  27.8 us
    dot_general x3, matrix products, linear_attention(): numer = jnp.einsum('cihe,chef->cihf', query, state, precision=best)  27.6 us
    all_to_all x1, waiting for transfers between devices, per_device(): lax.all_to_all(sent[0], 'dp', split_axis=0, concat_axis=0, tiled=True)  24.8 us
  transfers between devices with their start and end apart: 9, of which 6 were waited for; matrix products, arithmetic and copies ran while one was open for 17% of the time, Pallas kernels for 0%

commit v1 on v0

--- a/solution.py
+++ b/solution.py
@@ -119,7 +119,9 @@
     second_part = jnp.einsum(
         "tf,df->td", grad_hidden, up_weight, preferred_element_type=jnp.float32
     )
-    grad_second = lax.psum(second_part.astype(jnp.bfloat16), "tensor").astype(jnp.float32)
+    grad_second = jnp.sum(
+        lax.all_gather(second_part.astype(jnp.bfloat16), "tensor"), axis=0
+    ).astype(jnp.float32)
     middle_norm, grad_gain_second, grad_shift_second = second_pull(grad_second)
     grad_middle = grad_low.astype(jnp.float32) + middle_norm
     middle_low = grad_middle.astype(jnp.bfloat16)

time: 941 us -> 940 us (level)
    psum x1 -> x0, waiting for transfers between devices: 56.8 us -> none  [per_device(): lax.psum(second_part.astype(jnp.bfloat16), 'tensor').astype(jnp.float32)]
    all_gather x0 -> x1, waiting for transfers between devices: none -> 50.6 us  [per_device(): lax.all_gather(second_part.astype(jnp.bfloat16), 'tensor')]
where the time goes in v1:
time: 940 us; the launch traced here: 935 us
  waiting for transfers between devices  420 us (45%)
  local copies, waits for them, and re-layouts  190 us (20%)
  matrix products  148 us (16%)
  blocking collectives  60.4 us (6%)
  other arithmetic  59.1 us (6%)
  starting transfers between devices  42.2 us (4%)
  between operations  15.1 us (2%)
    psum x1, waiting for transfers between devices, per_device(): lax.psum((grad_qkv, grad_outproj, grad_up, grad_down, grad_up_bias, grad_...  165 us
    psum x1, waiting for transfers between devices, per_device(): lax.psum(ffn_part.astype(jnp.bfloat16), 'tensor').astype(jnp.float32)  108 us
    psum x1, blocking collectives, per_device(): lax.psum((grad_qkv, grad_outproj, grad_up, grad_down, grad_up_bias, grad_...  60.4 us
    psum x1, waiting for transfers between devices, per_device(): lax.psum(attn_part.astype(jnp.bfloat16), 'tensor').astype(jnp.float32)  53 us
    all_gather x1, waiting for transfers between devices, per_device(): lax.all_gather(second_part.astype(jnp.bfloat16), 'tensor')  50.6 us
    dot_general x3, matrix products, linear_attention(): jnp.einsum('chij,cjhf->cihf', scores, values, precision=best)  27.8 us
    dot_general x3, matrix products, linear_attention(): numer = jnp.einsum('cihe,chef->cihf', query, state, precision=best)  27.6 us
    all_to_all x1, waiting for transfers between devices, per_device(): lax.all_to_all(sent[0], 'dp', split_axis=0, concat_axis=0, tiled=True)  24.8 us
  transfers between devices with their start and end apart: 9, of which 6 were waited for; matrix products, arithmetic and copies ran while one was open for 17% of the time, Pallas kernels for 0%

profile of v1, /device:TPU:0, one launch (start us, length us, event | category | flops | bytes accessed | tf_op | source)
XLA Modules:
  0.0 934.7 jit_solution(4601692308884660456)
XLA Ops:
  13.1 20.6 %gather_fusion.1 = s32[2048]{0:T(1024)} fusion(s32[2048]{0:T(1024)S(1)} %copy-done.2, s32[2048]{0:T(1024)S(1)} %fusion.86), kind=kCustom, calls=%fused_computation.1 | custom fusion | bytes 24576 | tf_op jit(solution)/shard_map/gather | solution.py:81
  33.7 7.4 all-to-all-start.1
  41.0 9.2 gather_fusion
  56.3 11.1 %gather_fusion.5 = bf16[2048,512]{1,0:T(8,128)(2,1)} fusion(bf16[2048,512]{1,0:T(8,128)(2,1)} %param.16, s32[2048]{0:T(1024)S(1)} %fusion.86), kind=kCustom, calls=%fused_computation.5 | custom fusion | bytes 4202496 | tf_op jit(solution)/shard_map/gather | solution.py:80
  72.5 24.8 %all-to-all-done = bf16[16,128,512]{2,1,0:T(8,128)(2,1)S(1)} async-done(((bf16[16,128,512]{2,1,0:T(8,128)(2,1)}), bf16[16,128,512]{2,1,0:T(8,128)(2,1)S(1)}, u32[]{:S(2)}, u32[]{:S(2)}) %all-to-all-start) | async-done | bytes 2097184 | tf_op jit(solution)/shard_map/all_to_all | solution.py:84
  97.4 11.3 %all-to-all-start.3 = ((bf16[16,128,512]{2,1,0:T(8,128)(2,1)}), bf16[16,128,512]{2,1,0:T(8,128)(2,1)}, u32[]{:S(2)}, u32[]{:S(2)}) async-start(bf16[16,128,512]{2,1,0:T(8,128)(2,1)} %bitcast.115), calls=%async_computation.3 | async-start | bytes 4194304 | tf_op jit(solution)/shard_map/all_to_all | solution.py:85
  108.9 9.5 %gather_fusion.2 = bf16[2048,512]{1,0:T(8,128)(2,1)S(1)} fusion(bf16[2048,512]{1,0:T(8,128)(2,1)} %bitcast.114, s32[2048]{0:T(1024)S(1)} %fusion.87), kind=kCustom, calls=%fused_computation.2 | custom fusion | bytes 4202496 | tf_op jit(solution)/shard_map/gather | solution.py:90
  158.4 7.2 fusion.29
  178.8 11.3 %gather_fusion.6 = bf16[2048,512]{1,0:T(8,128)(2,1)} fusion(bf16[2048,512]{1,0:T(8,128)(2,1)} %bitcast.22, s32[2048]{0:T(1024)S(1)} %fusion.87), kind=kCustom, calls=%fused_computation.6 | custom fusion | bytes 4202496 | tf_op jit(solution)/shard_map/gather | solution.py:91
  190.1 53.0 %all-reduce.7.cloned.1.call-done = bf16[2048,512]{1,0:T(8,128)(2,1)} async-done(((bf16[2048,512]{1,0:T(8,128)(2,1)}), bf16[2048,512]{1,0:T(8,128)(2,1)}) %all-reduce.7.cloned.1.call-update) | async-done | bytes 2097168 | tf_op jit(solution)/shard_map/psum | solution.py:105
  269.6 50.6 %all-gather.3.cloned.1.call-done = bf16[4096,512]{1,0:T(8,128)(2,1)} async-done(((bf16[2048,512]{1,0:T(8,128)(2,1)}), bf16[4096,512]{1,0:T(8,128)(2,1)}) %all-gather.3.cloned.1.call-update) | async-done | bytes 4194320 | tf_op jit(solution)/shard_map/all_gather | solution.py:123
  342.4 15.5 %fusion.15 = f32[32,4,64,64]{3,2,1,0:T(8,128)} fusion(f32[32,4,64,64]{2,3,1,0:T(8,128)} %copy-done.30, f32[64,64]{0,1:T(8,128)S(1)} %fusion.79, f32[32,64,4,64]{1,0,3,2:T(8,128)} %reshape.276, f32[32,64,4]{1,2,0:T(4,128)S(1)} %copy-done.53), kind=kOutput, calls=%fused_computation.41 | convolution fusion | flops 403701760 | bytes 6340608 | tf_op jit(solution)/shard_map/transpose(jvp(chij,cjhf->cihf))/dot_general | solution.py:52
  357.9 13.6 %fusion.21 = f32[32,4,64,64]{2,3,1,0:T(8,128)} fusion(f32[32,4,64,64]{3,0,2,1:T(8,128)S(1)} %copy-done.23, f32[32,64,4,64]{1,0,3,2:T(8,128)S(1)} %copy-done.24, f32[32,64,4]{1,2,0:T(4,128)S(1)} %copy-done.53), kind=kOutput, calls=%fused_computation.47 | convolution fusion | flops 403177472 | bytes 6324224 | tf_op jit(solution)/shard_map/transpose(jvp(cihe,chef->cihf))/dot_general | solution.py:51
  378.4 7.5 fusion.19
  436.7 9.9 %add_bitcast_fusion = f32[32,64,4,64]{1,3,2,0:T(8,128)} fusion(f32[32,4,64,64]{2,3,1,0:T(8,128)} %fusion.21, f32[32,4,64,64]{2,3,1,0:T(8,128)} %fusion.19, f32[32,4,64]{2,1,0:T(4,128)S(1)} %copy.105, f32[32,4,64]{2,1,0:T(4,128)S(1)} %get-tuple-element.83, f32[64,64]{0,1:T(8,128)S(1)} %fusion.79, bf16[32,64,4,64]{3,2,1,0:T(4,128)(2,1)} %reshape.267), kind=kOutput, calls=%fused_computation.59 | convolution fusion | flops 405274624 | bytes 7421952 | tf_op jit(solution)/shard_map/transpose(jvp(cihe,cjhe->chij))/dot_general | solution.py:48
  467.3 107.7 %all-reduce.11.cloned.1.call-done = (bf16[2048,512]{1,0:T(8,128)(2,1)}, bf16[2048,512]{1,0:T(8,128)(2,1)}) async-done(((bf16[2048,512]{1,0:T(8,128)(2,1)}, bf16[2048,512]{1,0:T(8,128)(2,1)}), (bf16[2048,512]{1,0:T(8,128)(2,1)}, bf16[2048,512]{1,0:T(8,128)(2,1)})) %all-reduce.11.cloned.1.call-update) | async-done | bytes 4194320 | tf_op jit(solution)/shard_map/psum | solution.py:112
  587.9 11.1 %gather_fusion.7 = bf16[2048,512]{1,0:T(8,128)(2,1)} fusion(bf16[2048,512]{1,0:T(8,128)(2,1)} %get-tuple-element.80, s32[2048]{0:T(1024)S(1)} %broadcast_clamp_fusion), kind=kCustom, calls=%fused_computation.7 | custom fusion | bytes 4202496 | tf_op jit(solution)/shard_map/gather | solution.py:171
  615.7 11.1 %gather_fusion.3 = bf16[2048,512]{1,0:T(8,128)(2,1)} fusion(bf16[2048,512]{1,0:T(8,128)(2,1)} %get-tuple-element.81, s32[2048]{0:T(1024)S(1)} %broadcast_clamp_fusion), kind=kCustom, calls=%fused_computation.3 | custom fusion | bytes 4202496 | tf_op jit(solution)/shard_map/gather | solution.py:170
  626.9 19.3 %all-to-all-done.4 = bf16[16,128,512]{2,1,0:T(8,128)(2,1)} async-done(((bf16[16,128,512]{2,1,0:T(8,128)(2,1)}), bf16[16,128,512]{2,1,0:T(8,128)(2,1)}, u32[]{:S(2)}, u32[]{:S(2)}) %all-to-all-start.4) | async-done | bytes 2097184 | tf_op jit(solution)/shard_map/all_to_all | solution.py:175
  646.1 11.3 %all-to-all-start.2 = ((bf16[16,128,512]{2,1,0:T(8,128)(2,1)}), bf16[16,128,512]{2,1,0:T(8,128)(2,1)}, u32[]{:S(2)}, u32[]{:S(2)}) async-start(bf16[16,128,512]{2,1,0:T(8,128)(2,1)} %bitcast.116), calls=%async_computation.2 | async-start | bytes 4194304 | tf_op jit(solution)/shard_map/all_to_all | solution.py:174
  671.4 164.9 %all-reduce.9.cloned.1.call-done = (f32[3,512,256]{1,2,0:T(8,128)}, f32[256,512]{1,0:T(8,128)}, f32[512,1024]{1,0:T(8,128)}, f32[1024,512]{1,0:T(8,128)}) async-done(((f32[3,512,256]{1,2,0:T(8,128)}, f32[256,512]{1,0:T(8,128)}, f32[512,1024]{1,0:T(8,128)}, f32[1024,512]{1,0:T(8,128)}), (f32[3,512,256]{1,2,0:T(8,128)}, f32[256,512]{1,0:T(8,128)}, f32[512,1024]{1,0:T(8,128)}, ...) | async-done | bytes 6291472 | tf_op jit(solution)/shard_map/psum | solution.py:155
  839.4 60.4 %all-reduce = (f32[512]{0:T(512)}, f32[512]{0:T(512)}, f32[512]{0:T(512)}, f32[512]{0:T(512)}, f32[1024]{0:T(1024)}) all-reduce(f32[512]{0:T(512)S(1)} %get-tuple-element.52, f32[512]{0:T(512)S(1)} %get-tuple-element.55, f32[512]{0:T(512)S(1)} %get-tuple-element.50, ...), channel_id=1, replica_groups=mesh['dp'=16,'tensor'=2] {'dp'}, use_global_device_ids=true, to_apply=%region_23.24 | all-reduce | flops 3072 | bytes 24576 | tf_op jit(solution)/shard_map/psum | solution.py:155
  899.8 11.1 %gather_fusion.8 = bf16[2048,512]{1,0:T(8,128)(2,1)} fusion(bf16[2048,512]{1,0:T(8,128)(2,1)} %bitcast.38, s32[2048]{0:T(1024)S(1)} %fusion.88), kind=kCustom, calls=%fused_computation.8 | custom fusion | bytes 4202496 | tf_op jit(solution)/shard_map/gather | solution.py:179
  910.9 11.2 %gather_fusion.4 = bf16[2048,512]{1,0:T(8,128)(2,1)} fusion(bf16[2048,512]{1,0:T(8,128)(2,1)} %bitcast.20, s32[2048]{0:T(1024)S(1)} %fusion.88), kind=kCustom, calls=%fused_computation.4 | custom fusion | bytes 4202496 | tf_op jit(solution)/shard_map/gather | solution.py:178
  (238 shorter events, 249.3 us)
Async XLA Ops:
  7.2 33.9 %copy-start = (bf16[2048,512]{1,0:T(8,128)(2,1)S(1)}, bf16[2048,512]{1,0:T(8,128)(2,1)}, u32[]{:S(2)}) copy-start(bf16[2048,512]{1,0:T(8,128)(2,1)} %param.13) | copy-start | bytes 6291460
  13.1 20.6 %copy-start.54 = (s32[2048]{0:T(1024)}, s32[2048]{0:T(1024)S(1)}, u32[]{:S(2)}) copy-start(s32[2048]{0:T(1024)S(1)} %get-tuple-element.14) | copy-start | bytes 24580
  33.7 16.6 %all-to-all-start.1 = ((s32[16,1,128]{2,1,0:T(1,128)}), s32[16,1,128]{2,1,0:T(1,128)S(1)}, u32[]{:S(2)}, u32[]{:S(2)}) async-start(s32[16,1,128]{2,1,0:T(1,128)} %bitcast.2), calls=%async_computation.1 | async-start | bytes 16384 | tf_op jit(solution)/shard_map/all_to_all | solution.py:86
  50.2 17.2 %copy-start.50 = (s32[16,1,128]{2,1,0:T(1,128)}, s32[16,1,128]{2,1,0:T(1,128)S(1)}, u32[]{:S(2)}) copy-start(s32[16,1,128]{2,1,0:T(1,128)S(1)} %all-to-all-done.1) | copy-start | bytes 24580
  50.2 47.1 %all-to-all-start = ((bf16[16,128,512]{2,1,0:T(8,128)(2,1)}), bf16[16,128,512]{2,1,0:T(8,128)(2,1)S(1)}, u32[]{:S(2)}, u32[]{:S(2)}) async-start(bf16[16,128,512]{2,1,0:T(8,128)(2,1)} %bitcast.117), calls=%async_computation | async-start | bytes 4194304 | tf_op jit(solution)/shard_map/all_to_all | solution.py:84
  97.4 81.4 %all-to-all-start.3 = ((bf16[16,128,512]{2,1,0:T(8,128)(2,1)}), bf16[16,128,512]{2,1,0:T(8,128)(2,1)}, u32[]{:S(2)}, u32[]{:S(2)}) async-start(bf16[16,128,512]{2,1,0:T(8,128)(2,1)} %bitcast.115), calls=%async_computation.3 | async-start | bytes 4194304 | tf_op jit(solution)/shard_map/all_to_all | solution.py:85
  108.6 134.5 %all-reduce.7.cloned.1.call-start = ((), (), s32[]{:S(2)}) async-start(), calls=%async_computation.5 | async-start | bytes 4194304 | tf_op jit(solution)/shard_map/psum | solution.py:105
  178.8 141.4 %all-gather.3.cloned.1.call-start = ((), (), s32[]{:S(2)}) async-start(), calls=%async_computation.6 | async-start | bytes 6291456 | tf_op jit(solution)/shard_map/all_gather | solution.py:123
  190.1 56.5 %copy-start.58 = (f32[512]{0:T(512)S(1)}, f32[512]{0:T(512)}, u32[]{:S(2)}) copy-start(f32[512]{0:T(512)} %param.23) | copy-start | bytes 6148
  190.1 56.5 %copy-start.63 = (f32[1024]{0:T(1024)S(1)}, f32[1024]{0:T(1024)}, u32[]{:S(2)}) copy-start(f32[1024]{0:T(1024)} %param.25) | copy-start | bytes 12292
  190.1 56.5 %copy-start.64 = (f32[512]{0:T(512)S(1)}, f32[512]{0:T(512)}, u32[]{:S(2)}) copy-start(f32[512]{0:T(512)} %param.24) | copy-start | bytes 6148
  263.3 311.7 %all-reduce.11.cloned.1.call-start = ((), (), s32[]{:S(2)}) async-start(), calls=%async_computation.8 | async-start | bytes 8388608 | tf_op jit(solution)/shard_map/psum | solution.py:112
  342.4 15.5 %copy-start.23 = (f32[32,4,64,64]{3,0,2,1:T(8,128)S(1)}, f32[32,4,64,64]{3,0,2,1:T(8,128)}, u32[]{:S(2)}) copy-start(f32[32,4,64,64]{3,0,2,1:T(8,128)} %copy-done.22) | copy-start | bytes 6291460
  342.4 15.5 %copy-start.24 = (f32[32,64,4,64]{1,0,3,2:T(8,128)S(1)}, f32[32,64,4,64]{1,0,3,2:T(8,128)}, u32[]{:S(2)}) copy-start(f32[32,64,4,64]{1,0,3,2:T(8,128)} %reshape.276) | copy-start | bytes 6291460
  357.9 13.6 %copy-start.35 = (bf16[32,64,4,64]{1,3,2,0:T(8,128)(2,1)S(1)}, bf16[32,64,4,64]{1,3,2,0:T(8,128)(2,1)}, u32[]{:S(2)}) copy-start(bf16[32,64,4,64]{1,3,2,0:T(8,128)(2,1)} %copy.119) | copy-start | bytes 3145732
  466.6 108.4 %copy-start.45 = (f32[2048]{0:T(1024)S(1)}, f32[2048]{0:T(1024)}, u32[]{:S(2)}) copy-start(f32[2048]{0:T(1024)} %copy-done.44) | copy-start | bytes 24580
  466.6 108.4 %copy-start.57 = (f32[512]{0:T(512)S(1)}, f32[512]{0:T(512)}, u32[]{:S(2)}) copy-start(f32[512]{0:T(512)} %param.21) | copy-start | bytes 6148
  466.6 111.9 %copy-start.49 = (f32[2048]{0:T(1024)S(1)}, f32[2048]{0:T(1024)}, u32[]{:S(2)}) copy-start(f32[2048]{0:T(1024)} %copy-done.48) | copy-start | bytes 24580
  466.6 111.9 %copy-start.47 = (f32[2048]{0:T(1024)S(1)}, f32[2048]{0:T(1024)}, u32[]{:S(2)}) copy-start(f32[2048]{0:T(1024)} %copy-done.46) | copy-start | bytes 24580
  599.1 47.1 %all-to-all-start.4 = ((bf16[16,128,512]{2,1,0:T(8,128)(2,1)}), bf16[16,128,512]{2,1,0:T(8,128)(2,1)}, u32[]{:S(2)}, u32[]{:S(2)}) async-start(bf16[16,128,512]{2,1,0:T(8,128)(2,1)} %bitcast.118), calls=%async_computation.4 | async-start | bytes 4194304 | tf_op jit(solution)/shard_map/all_to_all | solution.py:175
  626.9 30.6 %copy-start.28 = (bf16[2048,256]{0,1:T(8,128)(2,1)S(1)}, bf16[2048,256]{0,1:T(8,128)(2,1)}, u32[]{:S(2)}) copy-start(bf16[2048,256]{0,1:T(8,128)(2,1)} %copy-done.27) | copy-start | bytes 3145732
  626.9 33.7 %copy-start.66 = (f32[512]{0:T(512)S(1)}, f32[512]{0:T(512)}, u32[]{:S(2)}) copy-start(f32[512]{0:T(512)} %param.22) | copy-start | bytes 6148
  646.1 264.8 %all-to-all-start.2 = ((bf16[16,128,512]{2,1,0:T(8,128)(2,1)}), bf16[16,128,512]{2,1,0:T(8,128)(2,1)}, u32[]{:S(2)}, u32[]{:S(2)}) async-start(bf16[16,128,512]{2,1,0:T(8,128)(2,1)} %bitcast.116), calls=%async_computation.2 | async-start | bytes 4194304 | tf_op jit(solution)/shard_map/all_to_all | solution.py:174
  657.4 178.9 %all-reduce.9.cloned.1.call-start = ((), (), s32[]{:S(2)}) async-start(), calls=%async_computation.7 | async-start | bytes 12582912 | tf_op jit(solution)/shard_map/psum | solution.py:155
  (55 other events, 278.1 us)
Sparse Core Ops, SparseCore 0:
  178.9 64.1 all-reduce.6
  263.4 56.7 all-gather.2
  466.7 108.2 all-reduce.10
  665.9 170.4 all-reduce.8
